TPU v7x, 32 devices: a whole 2x2x4 slice. The times are simulated.
32 devices in a mesh: fields: 2 (over x), prow: 8 (over z, y), pcol: 2 (over core).
Axes of the slice: x: 2, y: 2, z: 4, core: 2. Of those that a mesh axis runs over, the one named last changes fastest.
Arguments:
- inverse_tiles: bfloat16 [32, 16, 256, 256], P(('fields', 'prow'), 'pcol'), parts along dimension 0, may hold values from -6 to 6
- panel_blocks: bfloat16 [4, 8, 256, 512], P('fields', 'prow', None, 'pcol'), parts along dimension 0, may hold values from -0.125 to 0.125
- diag_inverse: float32 [4, 512], P('fields', 'pcol'), parts along dimension 0, may hold values from 0.5 to 2
- structure: int32 [4, 8], P('fields'), parts along dimension 0, may hold values from 0 to 15, as said below
- block_slot: int32 [32], P('fields'), parts along dimension 0, may hold values from 0 to 15, each once
Outputs:
- sigma_new: bfloat16 [4, 16, 256, 512], P('fields', 'prow', None, 'pcol'), parts along dimension 0
- variances: float32 [4, 512], P('fields', 'pcol'), parts along dimension 0
There are 2 independent parts, one for each index of `fields`. A program takes and returns all parts, laid end to end along the dimension named above; each array names one. Nothing has to cross between parts.
Inputs may be any that keep to these rules, and one draw needn't show every extreme that they name: `structure`: each row lists 8 distinct row blocks in increasing order, and the last is always 16 - 1. `block_slot`: each slot is used by exactly one row block.
All inputs are finite; a program needn't handle non-finite values.
Results may differ from a plain program's by a relative error of at most 0.0006.
Values may be sent and summed in bfloat16 or wider, within the bound.
No kernel may reach another device: no remote copies, remote signals or barrier semaphores. Data moves between devices by JAX's collectives and lax.ppermute only.
A program may use at most 128 MiB of HBM per device.

v0:
```python
import jax
import jax.numpy as jnp
from jax import lax
from jax.sharding import PartitionSpec as P


def swapped(shard, axis, stride):
    return lax.ppermute(shard, axis, [(i, i ^ 1 << stride) for i in range(lax.axis_size(axis))])


def make_accumulate(selected, row_hits, piece):
    contrib = jnp.einsum("iskxy,skyw->sixw", selected, piece, preferred_element_type=jnp.float32)
    own_panel = jnp.einsum("sik,skxw->sixw", row_hits, piece, preferred_element_type=jnp.float32)
    return (contrib, own_panel)


def per_device(inverse_tiles, panel_blocks, diag_inverse, structure, block_slot):
    rows_here = inverse_tiles.shape[0]
    tile_size = inverse_tiles.shape[2]
    supernodes = panel_blocks.shape[0]
    positions = structure.shape[1]
    prow_index = lax.axis_index("prow")
    pcol_index = lax.axis_index("pcol")
    slot_of = block_slot[structure]
    own_rows = prow_index * rows_here + jnp.arange(rows_here, dtype=jnp.int32)
    row_match = slot_of[:, None, :] == own_rows[None, :, None]
    row_hits = row_match.astype(jnp.bfloat16)
    row_used = jnp.any(row_match, axis=2)
    partner = swapped(inverse_tiles, "pcol", 0)
    first_half = jnp.where(pcol_index == 0, inverse_tiles, partner)
    second_half = jnp.where(pcol_index == 0, partner, inverse_tiles)
    whole_rows = jnp.concatenate([first_half, second_half], axis=1)
    selected = jnp.take(whole_rows, slot_of.reshape(-1), axis=1)
    selected = selected.reshape(rows_here, supernodes, positions, tile_size, tile_size)
    summed, own_panel = make_accumulate(
        selected, row_hits, lax.all_gather(panel_blocks, "prow", axis=1, tiled=True)
    )
    sigma_rows = jnp.where(row_used[:, :, None, None], -summed, jnp.zeros((), jnp.float32))
    partial_value = jnp.sum(own_panel * sigma_rows, axis=(1, 2))
    correction = lax.psum(partial_value, "prow")
    variances = diag_inverse - correction
    return (sigma_rows.astype(jnp.bfloat16), variances)


def solution(mesh):
    in_specs = (
        P(("fields", "prow"), "pcol", None, None),
        P("fields", "prow", None, "pcol"),
        P("fields", "pcol"),
        P("fields", None),
        P("fields"),
    )
    out_specs = (P("fields", "prow", None, "pcol"), P("fields", "pcol"))
    return jax.shard_map(
        per_device, mesh=mesh, in_specs=in_specs, out_specs=out_specs, check_vma=False
    )
```

profile of v0, /device:TPU:0, one launch (start us, length us, event | category | flops | bytes accessed | tf_op | source)
XLA Modules:
  0.0 95.9 jit_solution(17099047433927221169)
XLA Ops:
  7.2 0.0 copy-start
  7.2 0.0 all-gather.2.cloned.1.call-start
  7.2 0.7 all-gather.2.cloned.1.call-update
  7.9 0.6 collective-permute-start
  8.5 0.7 compare_select_fusion.1
  9.2 0.1 reshape.53
  9.2 0.0 copy-done
  9.2 0.7 gather_fusion
  9.9 0.1 reshape.52
  10.0 0.2 compare_reduce_fusion
  10.2 2.3 %collective-permute-done = bf16[2,8,256,256]{3,2,1,0:T(8,128)(2,1)S(1)} collective-permute-done((bf16[2,8,256,256]{3,2,1,0:T(8,128)(2,1)}, bf16[2,8,256,256]{3,2,1,0:T(8,128)(2,1)S(1)}, u32[]{:S(2)}, u32[]{:S(2)}) %collective-permute-start) | collective-permute-done | bytes 2097184 | tf_op jit(solution)/shard_map/ppermute | solution.py:8
  12.5 1.9 %broadcast_select_fusion.1 = (bf16[2,8,256,256]{3,2,1,0:T(8,128)(2,1)S(1)}, bf16[2,8,256,256]{3,2,1,0:T(8,128)(2,1)S(1)}) fusion(bf16[2,8,256,256]{3,2,1,0:T(8,128)(2,1)} %param.5, bf16[2,8,256,256]{3,2,1,0:T(8,128)(2,1)S(1)} %collective-permute-done, pred[]{:T(512)S(6)} %eq.20), kind=kLoop, calls=%fused_computation.11 | loop fusion | flops 2097152 | bytes 8388609 | tf_op jit(solution)/shard_map/jit(_where)/select_n | solution.py:30
  14.3 2.3 %pad_maximum_fusion = bf16[2,16,256,256]{3,2,1,0:T(8,128)(2,1)} fusion(bf16[2,8,256,256]{3,2,1,0:T(8,128)(2,1)S(1)} %get-tuple-element.3, bf16[2,8,256,256]{3,2,1,0:T(8,128)(2,1)S(1)} %get-tuple-element.2), kind=kLoop, calls=%fused_computation.2 | loop fusion | flops 2097152 | bytes 8388608 | tf_op jit(solution)/shard_map/concatenate | solution.py:32
  16.7 4.9 %gather_fusion.1 = bf16[16,2,256,256]{3,2,1,0:T(8,128)(2,1)} fusion(bf16[2,16,256,256]{3,2,1,0:T(8,128)(2,1)} %pad_maximum_fusion, s32[1024]{0:T(1024)S(1)} %pad_clamp_fusion), kind=kCustom, calls=%fused_computation.1 | custom fusion | bytes 8388672 | tf_op jit(solution)/shard_map/jit(_take)/gather | solution.py:33
  21.6 40.4 %all-gather.2.cloned.1.call-done = bf16[2,8,256,256]{3,2,1,0:T(8,128)(2,1)} async-done(((bf16[2,1,256,256]{3,2,1,0:T(8,128)(2,1)}), bf16[2,8,256,256]{3,2,1,0:T(8,128)(2,1)}) %all-gather.2.cloned.1.call-update) | async-done | bytes 2097168 | tf_op jit(solution)/shard_map/all_gather | solution.py:36
  62.0 0.0 copy-start.1
  62.0 3.2 %fusion.3 = f32[2,2,256,256]{3,1,2,0:T(2,128)S(1)} fusion(bf16[2,8,256,256]{3,2,1,0:T(8,128)(2,1)} %all-gather.2.cloned.1.call-done, s32[2,8]{1,0:T(2,128)S(1)} %reshape.52, s32[2]{0:T(128)S(1)} %iota_add_fusion), kind=kOutput, calls=%fused_computation.7 | convolution fusion | flops 4194336 | bytes 3145800 | tf_op jit(solution)/shard_map/sik,skxw->sixw/dot_general | solution.py:13
  65.2 0.0 copy-done.1
  65.2 0.0 copy-start.2
  65.2 4.3 %fusion.15 = (f32[2,256]{1,0:T(2,128)S(1)}, bf16[2,2,256,256]{3,2,1,0:T(8,128)(2,1)}) fusion(f32[2,2,256,256]{3,1,2,0:T(2,128)S(1)} %fusion.3, bf16[2,8,256,256]{3,2,1,0:T(8,128)(2,1)S(1)} %copy-done.1, bf16[2,2,8,256,256]{4,3,0,2,1:T(8,128)(2,1)} %bitcast.32, pred[2,8]{1,0:T(4,128)(4,1)S(1)} %compare_and_fusion, pred[2,2]{1,0:T(4,128)(4,1)S(1)} %compare_reduce_fusion), kind=kOutput, calls=%fused_computation.16 | convolution fusion | flops 1077149184 | bytes 7866388 | tf_op jit(solution)/shard_map/iskxy,skyw->sixw/dot_general | solution.py:12
  69.5 19.0 %psum.7 = f32[2,256]{1,0:T(2,128)S(1)} all-reduce(f32[2,256]{1,0:T(2,128)S(1)} %get-tuple-element.4), channel_id=1, replica_groups=mesh['fields'=2,'prow'=8,'pcol'=2] {'prow'}, use_global_device_ids=true, to_apply=%region_2.3 | all-reduce | flops 512 | bytes 4096 | tf_op jit(solution)/shard_map/psum | solution.py:40
  88.5 0.0 copy-done.2
  88.5 0.6 sub.3
  (5 shorter events, 0.0 us)
Async XLA Ops:
  7.2 2.1 %copy-start = (s32[16]{0:T(128)S(1)}, s32[16]{0:T(128)}, u32[]{:S(2)}) copy-start(s32[16]{0:T(128)} %param.9) | copy-start | bytes 196
  7.2 54.8 %all-gather.2.cloned.1.call-start = ((), (), s32[]{:S(2)}) async-start(), calls=%async_computation | async-start | bytes 2359296 | tf_op jit(solution)/shard_map/all_gather | solution.py:36
  7.9 4.6 %collective-permute-start = (bf16[2,8,256,256]{3,2,1,0:T(8,128)(2,1)}, bf16[2,8,256,256]{3,2,1,0:T(8,128)(2,1)S(1)}, u32[]{:S(2)}, u32[]{:S(2)}) collective-permute-start(bf16[2,8,256,256]{3,2,1,0:T(8,128)(2,1)} %param.5), channel_id=1, source_target_pairs={{0,1},{1,0},{2,3},{3,2},{4,5},{5,4},{6,7},{7,6},{8,9},{9,8},{10,11... | collective-permute-start | bytes 6291464 | tf_op jit(solution)/shard_map/ppermute | solution.py:8
  62.0 3.2 %copy-start.1 = (bf16[2,8,256,256]{3,2,1,0:T(8,128)(2,1)S(1)}, bf16[2,8,256,256]{3,2,1,0:T(8,128)(2,1)}, u32[]{:S(2)}) copy-start(bf16[2,8,256,256]{3,2,1,0:T(8,128)(2,1)} %all-gather.2.cloned.1.call-done) | copy-start | bytes 6291460
  65.2 23.3 %copy-start.2 = (f32[2,256]{1,0:T(2,128)S(1)}, f32[2,256]{1,0:T(2,128)}, u32[]{:S(2)}) copy-start(f32[2,256]{1,0:T(2,128)} %param.7) | copy-start | bytes 6148
Sparse Core Ops, SparseCore 0:
  10.2 51.7 all-gather.1
where the time goes:
time: 96.1 us; the launch traced here: 95.9 us
  waiting for transfers between devices  43.3 us (45%)
  blocking collectives  19 us (20%)
  between operations  14.1 us (15%)
  matrix products  7.51 us (8%)
  local copies, waits for them, and re-layouts  5.78 us (6%)
  other arithmetic  5.67 us (6%)
    all_gather x1, waiting for transfers between devices, per_device(): lax.all_gather(panel_blocks, 'prow', axis=1, tiled=True)  40.4 us
    psum x1, blocking collectives, per_device(): correction = lax.psum(partial_value, 'prow')  19 us
    gather x1, local copies, waits for them, and re-layouts, per_device(): selected = jnp.take(whole_rows, slot_of.reshape(-1), axis=1)  4.94 us
    dot_general x1, matrix products, make_accumulate(): jnp.einsum('iskxy,skyw->sixw', selected, piece, preferred_element_type=jn...  4.32 us
    dot_general x1, matrix products, make_accumulate(): jnp.einsum('sik,skxw->sixw', row_hits, piece, preferred_element_type=jnp....  3.19 us
    concatenate x1, other arithmetic, per_device(): whole_rows = jnp.concatenate([first_half, second_half], axis=1)  2.33 us
    ppermute x1, waiting for transfers between devices, swapped(): lax.ppermute(shard, axis, [(i, i ^ 1 << stride) for i in range(lax.axis_s...  2.26 us
  transfers between devices with their start and end apart: 2, of which 2 were waited for; matrix products, arithmetic and copies ran while one was open for 11% of the time, Pallas kernels for 0%

commit v1 on v0

--- a/solution.py
+++ b/solution.py
@@ -1,7 +1,31 @@
+import functools
 import jax
 import jax.numpy as jnp
 from jax import lax
 from jax.sharding import PartitionSpec as P
+
+
+def work_samples(u_in, mesh_ax):
+    parts_out = lax.axis_size(mesh_ax)
+    v_now = lax.axis_index(mesh_ax)
+    value_now, inter, v1 = (parts_out, v_now, u_in.shape[1])
+    m_next = jnp.zeros(
+        [pp * value_now if at == 1 else pp for at, pp in enumerate(u_in.shape)], u_in.dtype
+    )
+    everything = lax.dynamic_update_slice_in_dim(m_next, u_in, inter * v1, axis=1)
+    for i0 in range(1, value_now):
+        u_in = lax.ppermute(
+            u_in,
+            axis_name=mesh_ax,
+            perm=list(map(lambda at: (at, (at + 1) % value_now), range(value_now))),
+        )
+        everything = lax.dynamic_update_slice_in_dim(
+            everything, u_in, (inter - i0) % value_now * v1, axis=1
+        )
+    return everything
+
+
+_guide_counts = functools.partial(work_samples, mesh_ax="prow")
 
 
 def swapped(shard, axis, stride):
@@ -32,9 +56,7 @@
     whole_rows = jnp.concatenate([first_half, second_half], axis=1)
     selected = jnp.take(whole_rows, slot_of.reshape(-1), axis=1)
     selected = selected.reshape(rows_here, supernodes, positions, tile_size, tile_size)
-    summed, own_panel = make_accumulate(
-        selected, row_hits, lax.all_gather(panel_blocks, "prow", axis=1, tiled=True)
-    )
+    summed, own_panel = make_accumulate(selected, row_hits, _guide_counts(panel_blocks))
     sigma_rows = jnp.where(row_used[:, :, None, None], -summed, jnp.zeros((), jnp.float32))
     partial_value = jnp.sum(own_panel * sigma_rows, axis=(1, 2))
     correction = lax.psum(partial_value, "prow")

time: 96.1 us -> 162 us (1.69)
  local copies, waits for them, and re-layouts: 5.78 us -> 70 us
  between operations: 14.1 us -> 1.06 us
  waiting for transfers between devices: 43.3 us -> 54.9 us
  blocking collectives: 19 us -> 21.7 us
  starting transfers between devices: 0.6 us -> 3.07 us
  matrix products: 7.51 us -> 5.06 us
    dynamic_update_slice x0 -> x8, local copies, waits for them, and re-layouts: none -> 57.1 us  [the longest x7 49.9 us: work_samples(): lax.dynamic_update_slice_in_dim(everything, u_in, (inter - i0) % value_no...]
    ppermute x0 -> x7, waiting for transfers between devices: none -> 54.9 us  [work_samples(): lax.ppermute(u_in, axis_name=mesh_ax, perm=list(map(lambda at: (at, (at +...]
    all_gather x1 -> x0, waiting for transfers between devices: 40.4 us -> none  [per_device(): lax.all_gather(panel_blocks, 'prow', axis=1, tiled=True)]
    ppermute x0 -> x7, local copies, waits for them, and re-layouts: none -> 4.75 us  [work_samples(): lax.ppermute(u_in, axis_name=mesh_ax, perm=list(map(lambda at: (at, (at +...]
    ppermute x0 -> x7, starting transfers between devices: none -> 3.06 us  [work_samples(): lax.ppermute(u_in, axis_name=mesh_ax, perm=list(map(lambda at: (at, (at +...]
    psum x1, blocking collectives: 19 us -> 21.7 us  [per_device(): correction = lax.psum(partial_value, 'prow')]
    dot_general x1, matrix products: 3.19 us -> 0.76 us  [make_accumulate(): jnp.einsum('sik,skxw->sixw', row_hits, piece, preferred_element_type=jnp....]
    ppermute x1, waiting for transfers between devices: 2.26 us -> 0.01 us  [swapped(): lax.ppermute(shard, axis, [(i, i ^ 1 << stride) for i in range(lax.axis_s...]
  transfers between devices with their start and end apart: 2 -> 8, of which waited for: 2 -> 6; matrix products, arithmetic and copies ran while one was open for 11% -> 41% of each run, Pallas kernels for 0% -> 0%
where the time goes in v1:
time: 162 us; the launch traced here: 161 us
  local copies, waits for them, and re-layouts  70 us (43%)
  waiting for transfers between devices  54.9 us (34%)
  blocking collectives  21.7 us (13%)
  other arithmetic  5.64 us (3%)
  matrix products  5.06 us (3%)
  starting transfers between devices  3.07 us (2%)
    ppermute x7, waiting for transfers between devices, work_samples(): lax.ppermute(u_in, axis_name=mesh_ax, perm=list(map(lambda at: (at, (at +...  54.9 us
    dynamic_update_slice x7, local copies, waits for them, and re-layouts, work_samples(): lax.dynamic_update_slice_in_dim(everything, u_in, (inter - i0) % value_no...  49.9 us
    psum x1, blocking collectives, per_device(): correction = lax.psum(partial_value, 'prow')  21.7 us
    dynamic_update_slice x1, local copies, waits for them, and re-layouts, work_samples(): lax.dynamic_update_slice_in_dim(m_next, u_in, inter * v1, axis=1)  7.13 us
    gather x1, local copies, waits for them, and re-layouts, per_device(): selected = jnp.take(whole_rows, slot_of.reshape(-1), axis=1)  4.98 us
    ppermute x7, local copies, waits for them, and re-layouts, work_samples(): lax.ppermute(u_in, axis_name=mesh_ax, perm=list(map(lambda at: (at, (at +...  4.75 us
    dot_general x1, matrix products, make_accumulate(): jnp.einsum('iskxy,skyw->sixw', selected, piece, preferred_element_type=jn...  4.31 us
  transfers between devices with their start and end apart: 8, of which 6 were waited for; matrix products, arithmetic and copies ran while one was open for 41% of the time, Pallas kernels for 0%

profile of v1, /device:TPU:0, one launch (start us, length us, event | category | flops | bytes accessed | tf_op | source)
XLA Modules:
  0.0 161.4 jit_solution(7169499935429212717)
XLA Ops:
  0.6 0.0 copy-start
  0.6 3.0 %collective-permute-start.1 = (bf16[2,1,256,256]{3,2,1,0:T(8,128)(2,1)}, bf16[2,1,256,256]{3,2,1,0:T(8,128)(2,1)S(1)}, u32[]{:S(2)}, u32[]{:S(2)}) collective-permute-start(bf16[2,1,256,256]{3,2,1,0:T(8,128)(2,1)} %param.6), channel_id=1, source_target_pairs={{0,2},{2,4},{4,6},{6,8},{8,10},{10,12},{12,14},{14,0},{1,3},{3,5},... | collective-permute-start | bytes 786440 | tf_op jit(solution)/shard_map/ppermute | solution.py:17
  3.7 9.6 %collective-permute-done.1 = bf16[2,1,256,256]{3,2,1,0:T(8,128)(2,1)S(1)} collective-permute-done((bf16[2,1,256,256]{3,2,1,0:T(8,128)(2,1)}, bf16[2,1,256,256]{3,2,1,0:T(8,128)(2,1)S(1)}, u32[]{:S(2)}, u32[]{:S(2)}) %collective-permute-start.1) | collective-permute-done | bytes 262176 | tf_op jit(solution)/shard_map/ppermute | solution.py:17
  13.2 0.0 collective-permute-start.2
  13.3 0.0 collective-permute-start
  13.3 10.2 %collective-permute-done.2 = bf16[2,1,256,256]{3,2,1,0:T(8,128)(2,1)S(1)} collective-permute-done((bf16[2,1,256,256]{3,2,1,0:T(8,128)(2,1)S(1)}, bf16[2,1,256,256]{3,2,1,0:T(8,128)(2,1)S(1)}, u32[]{:S(2)}, u32[]{:S(2)}) %collective-permute-start.2) | collective-permute-done | bytes 262176 | tf_op jit(solution)/shard_map/ppermute | solution.py:17
  23.4 0.0 collective-permute-start.3
  23.4 9.3 %collective-permute-done.3 = bf16[2,1,256,256]{3,2,1,0:T(8,128)(2,1)S(1)} collective-permute-done((bf16[2,1,256,256]{3,2,1,0:T(8,128)(2,1)S(1)}, bf16[2,1,256,256]{3,2,1,0:T(8,128)(2,1)S(1)}, u32[]{:S(2)}, u32[]{:S(2)}) %collective-permute-start.3) | collective-permute-done | bytes 262176 | tf_op jit(solution)/shard_map/ppermute | solution.py:17
  32.7 0.0 collective-permute-start.4
  32.7 9.1 %collective-permute-done.4 = bf16[2,1,256,256]{3,2,1,0:T(8,128)(2,1)S(1)} collective-permute-done((bf16[2,1,256,256]{3,2,1,0:T(8,128)(2,1)S(1)}, bf16[2,1,256,256]{3,2,1,0:T(8,128)(2,1)S(1)}, u32[]{:S(2)}, u32[]{:S(2)}) %collective-permute-start.4) | collective-permute-done | bytes 262176 | tf_op jit(solution)/shard_map/ppermute | solution.py:17
  41.8 0.0 collective-permute-start.5
  41.8 0.7 compare_select_fusion.1
  42.5 0.1 reshape.53
  42.6 0.7 gather_fusion
  43.2 0.1 reshape.52
  43.3 7.5 %collective-permute-done.5 = bf16[2,1,256,256]{3,2,1,0:T(8,128)(2,1)S(1)} collective-permute-done((bf16[2,1,256,256]{3,2,1,0:T(8,128)(2,1)S(1)}, bf16[2,1,256,256]{3,2,1,0:T(8,128)(2,1)S(1)}, u32[]{:S(2)}, u32[]{:S(2)}) %collective-permute-start.5) | collective-permute-done | bytes 262176 | tf_op jit(solution)/shard_map/ppermute | solution.py:17
  50.9 0.0 collective-permute-start.6
  50.9 0.2 compare_reduce_fusion
  51.1 9.3 %collective-permute-done.6 = bf16[2,1,256,256]{3,2,1,0:T(8,128)(2,1)} collective-permute-done((bf16[2,1,256,256]{3,2,1,0:T(8,128)(2,1)S(1)}, bf16[2,1,256,256]{3,2,1,0:T(8,128)(2,1)}, u32[]{:S(2)}, u32[]{:S(2)}) %collective-permute-start.6) | collective-permute-done | bytes 262176 | tf_op jit(solution)/shard_map/ppermute | solution.py:17
  60.3 0.0 collective-permute-start.7
  60.5 1.4 copy.19
  61.9 0.1 broadcast_in_dim.35
  62.1 7.1 %dynamic_update_slice.24 = bf16[2,8,256,256]{3,1,2,0:T(8,128)(2,1)S(1)} dynamic-update-slice(bf16[2,8,256,256]{3,1,2,0:T(8,128)(2,1)S(1)} %broadcast_in_dim.35, bf16[2,1,256,256]{3,1,2,0:T(2,128)(2,1)S(1)} %copy.19, s32[]{:T(128)} %constant.72.clone.1, s32[]{:T(128)S(6)} %select_n.103, s32[]{:T(128)} %constant.72.clone.1, s32[]{:T(128)} %constant.72.clone.1) | dynamic-update-slice | bytes 524292 | tf_op jit(solution)/shard_map/dynamic_update_slice | solution.py:15
  69.2 0.4 copy.20
  69.6 7.1 %dynamic_update_slice.25 = bf16[2,8,256,256]{3,1,2,0:T(8,128)(2,1)S(1)} dynamic-update-slice(bf16[2,8,256,256]{3,1,2,0:T(8,128)(2,1)S(1)} %dynamic_update_slice.24, bf16[2,1,256,256]{3,1,2,0:T(2,128)(2,1)S(1)} %copy.20, s32[]{:T(128)} %constant.72.clone.1, s32[]{:T(128)S(6)} %select_n.105, s32[]{:T(128)} %constant.72.clone.1, s32[]{:T(128)} %constant.72.clone.1) | dynamic-update-slice | bytes 524292 | tf_op jit(solution)/shard_map/dynamic_update_slice | solution.py:22
  76.8 0.0 copy-start.3
  76.8 0.4 copy.21
  77.2 7.1 %dynamic_update_slice.26 = bf16[2,8,256,256]{3,1,2,0:T(8,128)(2,1)S(1)} dynamic-update-slice(bf16[2,8,256,256]{3,1,2,0:T(8,128)(2,1)S(1)} %dynamic_update_slice.25, bf16[2,1,256,256]{3,1,2,0:T(2,128)(2,1)S(1)} %copy.21, s32[]{:T(128)} %constant.72.clone.1, s32[]{:T(128)S(6)} %select_n.107, s32[]{:T(128)} %constant.72.clone.1, s32[]{:T(128)} %constant.72.clone.1) | dynamic-update-slice | bytes 524292 | tf_op jit(solution)/shard_map/dynamic_update_slice | solution.py:22
  84.4 0.4 copy.22
  84.8 7.1 %dynamic_update_slice.27 = bf16[2,8,256,256]{3,1,2,0:T(8,128)(2,1)S(1)} dynamic-update-slice(bf16[2,8,256,256]{3,1,2,0:T(8,128)(2,1)S(1)} %dynamic_update_slice.26, bf16[2,1,256,256]{3,1,2,0:T(2,128)(2,1)S(1)} %copy.22, s32[]{:T(128)} %constant.72.clone.1, s32[]{:T(128)S(6)} %select_n.109, s32[]{:T(128)} %constant.72.clone.1, s32[]{:T(128)} %constant.72.clone.1) | dynamic-update-slice | bytes 524292 | tf_op jit(solution)/shard_map/dynamic_update_slice | solution.py:22
  91.9 0.4 copy.23
  92.3 7.1 %dynamic_update_slice.28 = bf16[2,8,256,256]{3,1,2,0:T(8,128)(2,1)S(1)} dynamic-update-slice(bf16[2,8,256,256]{3,1,2,0:T(8,128)(2,1)S(1)} %dynamic_update_slice.27, bf16[2,1,256,256]{3,1,2,0:T(2,128)(2,1)S(1)} %copy.23, s32[]{:T(128)} %constant.72.clone.1, s32[]{:T(128)S(6)} %select_n.111, s32[]{:T(128)} %constant.72.clone.1, s32[]{:T(128)} %constant.72.clone.1) | dynamic-update-slice | bytes 524292 | tf_op jit(solution)/shard_map/dynamic_update_slice | solution.py:22
  99.5 0.4 copy.24
  99.9 7.1 %dynamic_update_slice.29 = bf16[2,8,256,256]{3,1,2,0:T(8,128)(2,1)S(1)} dynamic-update-slice(bf16[2,8,256,256]{3,1,2,0:T(8,128)(2,1)S(1)} %dynamic_update_slice.28, bf16[2,1,256,256]{3,1,2,0:T(2,128)(2,1)S(1)} %copy.24, s32[]{:T(128)} %constant.72.clone.1, s32[]{:T(128)S(6)} %select_n.113, s32[]{:T(128)} %constant.72.clone.1, s32[]{:T(128)} %constant.72.clone.1) | dynamic-update-slice | bytes 524292 | tf_op jit(solution)/shard_map/dynamic_update_slice | solution.py:22
  107.0 1.4 copy.25
  108.4 7.1 %dynamic_update_slice.30 = bf16[2,8,256,256]{3,1,2,0:T(8,128)(2,1)S(1)} dynamic-update-slice(bf16[2,8,256,256]{3,1,2,0:T(8,128)(2,1)S(1)} %dynamic_update_slice.29, bf16[2,1,256,256]{3,1,2,0:T(2,128)(2,1)S(1)} %copy.25, s32[]{:T(128)} %constant.72.clone.1, s32[]{:T(128)S(6)} %select_n.115, s32[]{:T(128)} %constant.72.clone.1, s32[]{:T(128)} %constant.72.clone.1) | dynamic-update-slice | bytes 524292 | tf_op jit(solution)/shard_map/dynamic_update_slice | solution.py:22
  115.5 0.0 collective-permute-done.7
  115.6 1.4 copy.26
  116.9 7.1 %dynamic_update_slice.31 = bf16[2,8,256,256]{3,1,2,0:T(8,128)(2,1)S(1)} dynamic-update-slice(bf16[2,8,256,256]{3,1,2,0:T(8,128)(2,1)S(1)} %dynamic_update_slice.30, bf16[2,1,256,256]{3,1,2,0:T(2,128)(2,1)S(1)} %copy.26, s32[]{:T(128)} %constant.72.clone.1, s32[]{:T(128)S(6)} %select_n.117, s32[]{:T(128)} %constant.72.clone.1, s32[]{:T(128)} %constant.72.clone.1) | dynamic-update-slice | bytes 524292 | tf_op jit(solution)/shard_map/dynamic_update_slice | solution.py:22
  124.1 0.0 copy-start.1
  124.1 0.8 fusion.14
  124.8 0.8 copy-done.1
  125.7 1.9 %broadcast_select_fusion.1 = (bf16[2,8,256,256]{3,2,1,0:T(8,128)(2,1)S(1)}, bf16[2,8,256,256]{3,2,1,0:T(8,128)(2,1)S(1)}) fusion(bf16[2,8,256,256]{3,2,1,0:T(8,128)(2,1)S(1)} %copy-done.1, bf16[2,8,256,256]{3,2,1,0:T(8,128)(2,1)} %collective-permute-done, pred[]{:T(512)S(6)} %eq.28), kind=kLoop, calls=%fused_computation.9 | loop fusion | flops 2097152 | bytes 8388609 | tf_op jit(solution)/shard_map/jit(_where)/select_n | solution.py:54
  127.5 2.3 %pad_maximum_fusion = bf16[2,16,256,256]{3,2,1,0:T(8,128)(2,1)} fusion(bf16[2,8,256,256]{3,2,1,0:T(8,128)(2,1)S(1)} %get-tuple-element.3, bf16[2,8,256,256]{3,2,1,0:T(8,128)(2,1)S(1)} %get-tuple-element.2), kind=kLoop, calls=%fused_computation.2 | loop fusion | flops 2097152 | bytes 8388608 | tf_op jit(solution)/shard_map/concatenate | solution.py:56
  129.8 5.0 %gather_fusion.1 = bf16[16,2,256,256]{3,2,1,0:T(8,128)(2,1)} fusion(bf16[2,16,256,256]{3,2,1,0:T(8,128)(2,1)} %pad_maximum_fusion, s32[1024]{0:T(1024)S(1)} %pad_clamp_fusion), kind=kCustom, calls=%fused_computation.1 | custom fusion | bytes 8388672 | tf_op jit(solution)/shard_map/jit(_take)/gather | solution.py:57
  134.8 4.3 %fusion.13 = (f32[2,256]{1,0:T(2,128)S(1)}, bf16[2,2,256,256]{3,2,1,0:T(8,128)(2,1)}) fusion(f32[2,2,256,256]{3,1,2,0:T(2,128)S(1)} %fusion.14, bf16[2,8,256,256,1]{3,1,2,0,4:T(8,128)(2,1)S(1)} %bitcast.21, bf16[2,2,8,256,256]{4,3,0,2,1:T(8,128)(2,1)} %bitcast.22, pred[2,8]{1,0:T(4,128)(4,1)S(1)} %compare_and_fusion, pred[2,2]{1,0:T(4,128)(4,1)S(1)} %compare_reduce_fusion), kind=kOutput, calls=%fused_computation.14 | convolution fusion | flops 1077149184 | bytes 7866388 | tf_op jit(solution)/shard_map/iskxy,skyw->sixw/dot_general | solution.py:36
  139.1 21.7 %psum.7 = f32[2,256]{1,0:T(2,128)S(1)} all-reduce(f32[2,256]{1,0:T(2,128)S(1)} %get-tuple-element.4), channel_id=1, replica_groups=mesh['fields'=2,'prow'=8,'pcol'=2] {'prow'}, use_global_device_ids=true, to_apply=%region_2.3 | all-reduce | flops 512 | bytes 4096 | tf_op jit(solution)/shard_map/psum | solution.py:62
  160.8 0.6 sub.31
  (16 shorter events, 0.0 us)
Async XLA Ops:
  0.6 42.0 %copy-start = (s32[16]{0:T(128)S(1)}, s32[16]{0:T(128)}, u32[]{:S(2)}) copy-start(s32[16]{0:T(128)} %param.9) | copy-start | bytes 196
  0.6 12.6 %collective-permute-start.1 = (bf16[2,1,256,256]{3,2,1,0:T(8,128)(2,1)}, bf16[2,1,256,256]{3,2,1,0:T(8,128)(2,1)S(1)}, u32[]{:S(2)}, u32[]{:S(2)}) collective-permute-start(bf16[2,1,256,256]{3,2,1,0:T(8,128)(2,1)} %param.6), channel_id=1, source_target_pairs={{0,2},{2,4},{4,6},{6,8},{8,10},{10,12},{12,14},{14,0},{1,3},{3,5},... | collective-permute-start | bytes 786440 | tf_op jit(solution)/shard_map/ppermute | solution.py:17
  13.2 10.2 %collective-permute-start.2 = (bf16[2,1,256,256]{3,2,1,0:T(8,128)(2,1)S(1)}, bf16[2,1,256,256]{3,2,1,0:T(8,128)(2,1)S(1)}, u32[]{:S(2)}, u32[]{:S(2)}) collective-permute-start(bf16[2,1,256,256]{3,2,1,0:T(8,128)(2,1)S(1)} %collective-permute-done.1), channel_id=1, source_target_pairs={{0,2},{2,4},{4,6},{6,8},{8,10},{10,12},{12,14},{14,0},{1,3},{3,5},... | collective-permute-start | bytes 786440 | tf_op jit(solution)/shard_map/ppermute | solution.py:17
  13.3 111.6 %collective-permute-start = (bf16[2,8,256,256]{3,2,1,0:T(8,128)(2,1)}, bf16[2,8,256,256]{3,2,1,0:T(8,128)(2,1)}, u32[]{:S(2)}, u32[]{:S(2)}) collective-permute-start(bf16[2,8,256,256]{3,2,1,0:T(8,128)(2,1)} %param.5), channel_id=1, source_target_pairs={{0,1},{1,0},{2,3},{3,2},{4,5},{5,4},{6,7},{7,6},{8,9},{9,8},{10,11... | collective-permute-start | bytes 6291464 | tf_op jit(solution)/shard_map/ppermute | solution.py:32
  23.4 9.3 %collective-permute-start.3 = (bf16[2,1,256,256]{3,2,1,0:T(8,128)(2,1)S(1)}, bf16[2,1,256,256]{3,2,1,0:T(8,128)(2,1)S(1)}, u32[]{:S(2)}, u32[]{:S(2)}) collective-permute-start(bf16[2,1,256,256]{3,2,1,0:T(8,128)(2,1)S(1)} %collective-permute-done.2), channel_id=1, source_target_pairs={{0,2},{2,4},{4,6},{6,8},{8,10},{10,12},{12,14},{14,0},{1,3},{3,5},... | collective-permute-start | bytes 786440 | tf_op jit(solution)/shard_map/ppermute | solution.py:17
  32.7 9.1 %collective-permute-start.4 = (bf16[2,1,256,256]{3,2,1,0:T(8,128)(2,1)S(1)}, bf16[2,1,256,256]{3,2,1,0:T(8,128)(2,1)S(1)}, u32[]{:S(2)}, u32[]{:S(2)}) collective-permute-start(bf16[2,1,256,256]{3,2,1,0:T(8,128)(2,1)S(1)} %collective-permute-done.3), channel_id=1, source_target_pairs={{0,2},{2,4},{4,6},{6,8},{8,10},{10,12},{12,14},{14,0},{1,3},{3,5},... | collective-permute-start | bytes 786440 | tf_op jit(solution)/shard_map/ppermute | solution.py:17
  41.8 20.1 %copy-start.2 = (bf16[2,1,256,256]{3,2,1,0:T(8,128)(2,1)}, bf16[2,1,256,256]{3,2,1,0:T(8,128)(2,1)S(1)}, u32[]{:S(2)}) copy-start(bf16[2,1,256,256]{3,2,1,0:T(8,128)(2,1)S(1)} %collective-permute-done.4) | copy-start | bytes 786436
  41.8 9.1 %collective-permute-start.5 = (bf16[2,1,256,256]{3,2,1,0:T(8,128)(2,1)S(1)}, bf16[2,1,256,256]{3,2,1,0:T(8,128)(2,1)S(1)}, u32[]{:S(2)}, u32[]{:S(2)}) collective-permute-start(bf16[2,1,256,256]{3,2,1,0:T(8,128)(2,1)S(1)} %collective-permute-done.4), channel_id=1, source_target_pairs={{0,2},{2,4},{4,6},{6,8},{8,10},{10,12},{12,14},{14,0},{1,3},{3,5},... | collective-permute-start | bytes 786440 | tf_op jit(solution)/shard_map/ppermute | solution.py:17
  50.9 11.0 %copy-start.4 = (bf16[2,1,256,256]{3,2,1,0:T(8,128)(2,1)}, bf16[2,1,256,256]{3,2,1,0:T(8,128)(2,1)S(1)}, u32[]{:S(2)}) copy-start(bf16[2,1,256,256]{3,2,1,0:T(8,128)(2,1)S(1)} %collective-permute-done.5) | copy-start | bytes 786436
  50.9 9.5 %collective-permute-start.6 = (bf16[2,1,256,256]{3,2,1,0:T(8,128)(2,1)S(1)}, bf16[2,1,256,256]{3,2,1,0:T(8,128)(2,1)}, u32[]{:S(2)}, u32[]{:S(2)}) collective-permute-start(bf16[2,1,256,256]{3,2,1,0:T(8,128)(2,1)S(1)} %collective-permute-done.5), channel_id=1, source_target_pairs={{0,2},{2,4},{4,6},{6,8},{8,10},{10,12},{12,14},{14,0},{1,3},{3,5},... | collective-permute-start | bytes 786440 | tf_op jit(solution)/shard_map/ppermute | solution.py:17
  60.3 55.2 %collective-permute-start.7 = (bf16[2,1,256,256]{3,2,1,0:T(8,128)(2,1)}, bf16[2,1,256,256]{3,2,1,0:T(8,128)(2,1)}, u32[]{:S(2)}, u32[]{:S(2)}) collective-permute-start(bf16[2,1,256,256]{3,2,1,0:T(8,128)(2,1)} %collective-permute-done.6), channel_id=1, source_target_pairs={{0,2},{2,4},{4,6},{6,8},{8,10},{10,12},{12,14},{14,0},{1,3},{3,5},... | collective-permute-start | bytes 786440 | tf_op jit(solution)/shard_map/ppermute | solution.py:17
  76.8 15.1 %copy-start.3 = (bf16[2,1,256,256]{3,2,1,0:T(8,128)(2,1)S(1)}, bf16[2,1,256,256]{3,2,1,0:T(8,128)(2,1)}, u32[]{:S(2)}) copy-start(bf16[2,1,256,256]{3,2,1,0:T(8,128)(2,1)} %copy-done.2) | copy-start | bytes 786436
  84.3 15.1 %copy-start.5 = (bf16[2,1,256,256]{3,2,1,0:T(8,128)(2,1)S(1)}, bf16[2,1,256,256]{3,2,1,0:T(8,128)(2,1)}, u32[]{:S(2)}) copy-start(bf16[2,1,256,256]{3,2,1,0:T(8,128)(2,1)} %copy-done.4) | copy-start | bytes 786436
  124.1 1.6 copy-start.1
  134.8 26.0 %copy-start.6 = (f32[2,256]{1,0:T(2,128)S(1)}, f32[2,256]{1,0:T(2,128)}, u32[]{:S(2)}) copy-start(f32[2,256]{1,0:T(2,128)} %param.7) | copy-start | bytes 6148
